TPU v7x, 32 devices: a whole 2x2x4 slice. The times are simulated.
32 devices in a mesh: rows: 4 (over x, core), feat: 8 (over z, y).
Axes of the slice: x: 2, y: 2, z: 4, core: 2. Of those that a mesh axis runs over, the one named last changes fastest.
Arguments:
- embeddings: bfloat16 [512, 1024], P(('rows', 'feat')), may hold values from -12 to 12
- freqs: bfloat16 [1024, 65536], P(None, 'feat'), may hold values from -0.1875 to 0.1875
- phases: float32 [65536], P('feat'), may hold values from 0 to 6.2831855
- sketch: bfloat16 [65536, 256], P('feat'), may hold values from -0.0234375 to 0.0234375
Outputs:
- basis: float32 [512, 256], P(('rows', 'feat'))
- coeffs: float32 [256, 65536], P(None, 'feat')
All inputs are finite; a program needn't handle non-finite values.
Results may differ from a plain program's by a relative error of at most 0.0048.
Values may be sent and summed in bfloat16 or wider, within the bound.
A program may use at most 128 MiB of HBM per device.

v0:
```python
import jax
import jax.numpy as jnp
from jax import lax
from jax.sharding import PartitionSpec as P


def per_device(embeddings, freqs, phases, sketch):
    rows_dev = embeddings.shape[0]
    row_count = rows_dev * lax.axis_size("feat") * lax.axis_size("rows")
    mixed = jnp.dot(
        lax.all_gather(embeddings, "feat", axis=0, tiled=True),
        freqs,
        preferred_element_type=jnp.float32,
    )
    features = jnp.cos(mixed + phases).astype(jnp.bfloat16)
    owned_rows = lax.psum_scatter(
        jnp.dot(features, sketch, preferred_element_type=jnp.float32),
        "feat",
        scatter_dimension=0,
        tiled=True,
    )
    local_gram = jnp.dot(owned_rows.T, owned_rows, precision=lax.Precision.HIGHEST)
    gram_matrix = lax.psum(local_gram, ("rows", "feat")) / row_count
    factor = jnp.linalg.cholesky(gram_matrix)
    basis = jax.scipy.linalg.solve_triangular(factor, owned_rows.T, lower=True).T
    block_basis = lax.all_gather(basis.astype(jnp.bfloat16), "feat", axis=0, tiled=True)
    partial_value = lax.dot_general(
        block_basis, features, (((0,), (0,)), ((), ())), preferred_element_type=jnp.float32
    )
    coeffs = lax.psum(partial_value, "rows") / row_count
    return (basis, coeffs)


def solution(mesh):
    placed = (P(("rows", "feat"), None), P(None, "feat"), P("feat"), P("feat", None))
    return jax.shard_map(
        per_device,
        mesh=mesh,
        in_specs=placed,
        out_specs=(P(("rows", "feat"), None), P(None, "feat")),
        check_vma=False,
    )
```

profile of v0, /device:TPU:0, one launch (start us, length us, event | category | flops | bytes accessed | tf_op | source)
XLA Modules:
  0.0 516.5 jit_solution(3243274491165157878)
XLA Ops:
  7.2 0.0 reduce-scatter.2.cloned.1.call-start
  7.2 32.7 %all_gather.6 = bf16[128,1024]{1,0:T(8,128)(2,1)S(1)} all-gather(bf16[16,1024]{1,0:T(8,128)(2,1)} %param.4), channel_id=1, replica_groups=mesh['rows'=4,'feat'=8] {'feat'}, dimensions={0}, use_global_device_ids=true | all-gather | bytes 294912 | tf_op jit(solution)/shard_map/all_gather | solution.py:11
  39.9 0.0 copy-start
  40.0 18.1 %fusion.1 = bf16[128,8192]{1,0:T(8,128)(2,1)S(1)} fusion(bf16[128,1024]{1,0:T(8,128)(2,1)S(1)} %all_gather.6, bf16[1024,8192]{1,0:T(8,128)(2,1)} %param.5, f32[8192]{0:T(1024)} %param.6), kind=kOutput, calls=%fused_computation.4 | convolution fusion | flops 2149580800 | bytes 19169280 | tf_op jit(solution)/shard_map/dot_general | solution.py:10
  58.1 0.0 copy-done
  58.1 1.5 fusion.12
  59.6 0.0 reduce-scatter.2.cloned.1.call-update
  59.6 0.0 all-reduce.4.cloned.1.call-start
  59.6 62.0 %reduce-scatter.2.cloned.1.call-done = f32[16,256]{1,0:T(8,128)} async-done(((f32[128,256]{1,0:T(8,128)}), f32[16,256]{1,0:T(8,128)}) %reduce-scatter.2.cloned.1.call-update) | async-done | bytes 16400 | tf_op jit(solution)/shard_map/reduce_scatter | solution.py:16
  121.6 0.0 copy-start.1
  121.6 1.9 fusion.13
  123.6 0.0 all-reduce.4.cloned.1.call-update
  123.6 0.2 all-reduce.6.cloned.1.call-start
  123.8 128.0 %all-reduce.4.cloned.1.call-done = f32[256,256]{0,1:T(8,128)} async-done(((f32[256,256]{0,1:T(8,128)}), f32[256,256]{0,1:T(8,128)}) %all-reduce.4.cloned.1.call-update) | async-done | bytes 262160 | tf_op jit(solution)/shard_map/psum | solution.py:23
  251.8 1.0 broadcast_multiply_fusion.1
  252.8 0.1 copy.7
  252.9 1.0 fusion.2
  253.9 11.7 %cholesky.50 = f32[128,128]{1,0:T(8,128)S(1)} custom-call(f32[128,128]{1,0:T(8,128)S(1)} %cholesky.118), custom_call_target="Cholesky" | custom-call | tf_op jit(solution)/shard_map/jit(cholesky)/cholesky | solution.py:24
  265.7 9.8 %custom-call.15 = f32[1,128,128]{1,2,0:T(8,128)S(1)} custom-call(f32[1,128,128]{2,1,0:T(8,128)S(1)} %get-tuple-element.25), custom_call_target="InvertDiagBlocksLowerTriangular" | custom-call | tf_op jit(solution)/shard_map/jit(cholesky)/cholesky | solution.py:24
  275.5 0.2 constant_dynamic-update-slice_fusion.1
  275.7 0.3 convolution_subtract_fusion
  276.0 11.7 %cholesky.105 = f32[128,128]{1,0:T(8,128)S(1)} custom-call(f32[128,128]{1,0:T(8,128)S(1)} %convolution_subtract_fusion), custom_call_target="Cholesky" | custom-call | tf_op jit(solution)/shard_map/jit(cholesky)/cholesky | solution.py:24
  287.8 0.7 compare_reduce_fusion
  289.9 0.1 triangular_solve.57
  289.9 4.3 while.1
  290.1 0.6 fusion.28
  290.7 1.4 bitcast_dynamic-update-slice_fusion.2
  292.2 0.6 fusion.28
  292.8 1.4 bitcast_dynamic-update-slice_fusion.2
  294.2 19.7 %custom-call.16 = f32[2,128,128]{1,2,0:T(8,128)S(1)} custom-call(f32[2,128,128]{2,1,0:T(8,128)S(1)} %get-tuple-element.9), custom_call_target="InvertDiagBlocksLowerTriangular" | custom-call | tf_op jit(solution)/shard_map/jit(_solve_triangular)/triangular_solve | solution.py:25
  313.9 0.0 copy-done.1
  313.9 0.2 fusion.5
  314.1 0.2 convolution_subtract_fusion.1
  314.3 0.2 fusion.4
  314.5 0.6 fusion.10
  315.1 30.5 %all_gather.7 = bf16[128,256]{1,0:T(8,128)(2,1)S(1)} all-gather(bf16[16,256]{1,0:T(8,128)(2,1)S(1)} %get-tuple-element.18), channel_id=1, replica_groups=mesh['rows'=4,'feat'=8] {'feat'}, dimensions={0}, use_global_device_ids=true | all-gather | bytes 73728 | tf_op jit(solution)/shard_map/all_gather | solution.py:26
  345.6 4.7 fusion.14
  350.3 0.0 all-reduce.6.cloned.1.call-update
  350.3 152.0 %all-reduce.6.cloned.1.call-done = f32[256,8192]{1,0:T(8,128)} async-done(((f32[256,8192]{1,0:T(8,128)}), f32[256,8192]{1,0:T(8,128)}) %all-reduce.6.cloned.1.call-update) | async-done | bytes 8388624 | tf_op jit(solution)/shard_map/psum | solution.py:30
  502.3 7.7 %broadcast_multiply_fusion = f32[256,8192]{1,0:T(8,128)} fusion(f32[256,8192]{1,0:T(8,128)} %all-reduce.6.cloned.1.call-done), kind=kLoop, calls=%fused_computation.5 | loop fusion | flops 2097152 | bytes 16777216 | tf_op jit(solution)/shard_map/div | solution.py:30
  (9 shorter events, 0.1 us)
Async XLA Ops:
  7.2 114.5 %reduce-scatter.2.cloned.1.call-start = ((), (), s32[]{:S(2)}) async-start(), calls=%async_computation.1 | async-start | bytes 147456 | tf_op jit(solution)/shard_map/reduce_scatter | solution.py:16
  39.9 18.2 %copy-start = (bf16[8192,256]{1,0:T(8,128)(2,1)S(1)}, bf16[8192,256]{1,0:T(8,128)(2,1)}, u32[]{:S(2)}) copy-start(bf16[8192,256]{1,0:T(8,128)(2,1)} %param.7) | copy-start | bytes 12582916
  59.6 192.2 %all-reduce.4.cloned.1.call-start = ((), (), s32[]{:S(2)}) async-start(), calls=%async_computation.2 | async-start | bytes 524288 | tf_op jit(solution)/shard_map/psum | solution.py:23
  121.6 192.3 %copy-start.1 = (f32[16,256]{1,0:T(8,128)S(1)}, f32[16,256]{1,0:T(8,128)}, u32[]{:S(2)}) copy-start(f32[16,256]{1,0:T(8,128)} %reduce-scatter.2.cloned.1.call-done) | copy-start | bytes 49156
  123.6 378.7 %all-reduce.6.cloned.1.call-start = ((), (), s32[]{:S(2)}) async-start(), calls=%async_computation.3 | async-start | bytes 16777216 | tf_op jit(solution)/shard_map/psum | solution.py:30
Sparse Core Ops, SparseCore 0:
  59.7 61.8 reduce-scatter.1
  127.7 124.0 all-reduce.3
  350.4 151.8 all-reduce.5
where the time goes:
time: 517 us
  waiting for transfers between devices  342 us (66%)
  other arithmetic  64 us (12%)
  blocking collectives  63.2 us (12%)
  matrix products  27.2 us (5%)
  between operations  15.2 us (3%)
    psum x1, waiting for transfers between devices, per_device(): coeffs = lax.psum(partial_value, 'rows') / row_count  152 us
    psum x1, waiting for transfers between devices, per_device(): gram_matrix = lax.psum(local_gram, ('rows', 'feat')) / row_count  128 us
    reduce_scatter x1, waiting for transfers between devices, per_device(): lax.psum_scatter(jnp.dot(features, sketch, preferred_element_type=jnp.flo...  62 us
    another operation x6, other arithmetic, per_device(): factor = jnp.linalg.cholesky(gram_matrix)  34 us
    all_gather x1, blocking collectives, per_device(): lax.all_gather(embeddings, 'feat', axis=0, tiled=True)  32.7 us
    all_gather x1, blocking collectives, per_device(): lax.all_gather(basis.astype(jnp.bfloat16), 'feat', axis=0, tiled=True)  30.5 us
    another operation x3, other arithmetic, per_device(): jax.scipy.linalg.solve_triangular(factor, owned_rows.T, lower=True)  19.7 us
    dot_general x1, matrix products, per_device(): jnp.dot(lax.all_gather(embeddings, 'feat', axis=0, tiled=True), freqs, pr...  18.1 us
  transfers between devices with their start and end apart: 3, of which 3 were waited for; matrix products, arithmetic and copies ran while one was open for 0% of the time, Pallas kernels for 0%

commit v1 on v0

--- a/solution.py
+++ b/solution.py
@@ -27,7 +27,12 @@
     partial_value = lax.dot_general(
         block_basis, features, (((0,), (0,)), ((), ())), preferred_element_type=jnp.float32
     )
-    coeffs = lax.psum(partial_value, "rows") / row_count
+
+    def prepare_face_now(unit):
+        last = lax.all_gather(unit, axis_name="rows")
+        return jnp.sum(last, axis=0)
+
+    coeffs = prepare_face_now(partial_value) / row_count
     return (basis, coeffs)
 
 

time: 517 us -> 581 us (1.12)
  waiting for transfers between devices: 342 us -> 391 us
  other arithmetic: 64 us -> 79.9 us
    all_gather x0 -> x1, waiting for transfers between devices: none -> 201 us  [prepare_face_now(): last = lax.all_gather(unit, axis_name='rows')]
    psum x1 -> x0, waiting for transfers between devices: 152 us -> none  [per_device(): coeffs = lax.psum(partial_value, 'rows') / row_count]
    reduce_sum x0 -> x1, other arithmetic: none -> 15.9 us  [prepare_face_now(): return jnp.sum(last, axis=0)]
where the time goes in v1:
time: 581 us
  waiting for transfers between devices  391 us (67%)
  other arithmetic  79.9 us (14%)
  blocking collectives  63.2 us (11%)
  matrix products  27.2 us (5%)
  between operations  15.2 us (3%)
    all_gather x1, waiting for transfers between devices, prepare_face_now(): last = lax.all_gather(unit, axis_name='rows')  201 us
    psum x1, waiting for transfers between devices, per_device(): gram_matrix = lax.psum(local_gram, ('rows', 'feat')) / row_count  128 us
    reduce_scatter x1, waiting for transfers between devices, per_device(): lax.psum_scatter(jnp.dot(features, sketch, preferred_element_type=jnp.flo...  62 us
    another operation x6, other arithmetic, per_device(): factor = jnp.linalg.cholesky(gram_matrix)  34 us
    all_gather x1, blocking collectives, per_device(): lax.all_gather(embeddings, 'feat', axis=0, tiled=True)  32.7 us
    all_gather x1, blocking collectives, per_device(): lax.all_gather(basis.astype(jnp.bfloat16), 'feat', axis=0, tiled=True)  30.5 us
    another operation x3, other arithmetic, per_device(): jax.scipy.linalg.solve_triangular(factor, owned_rows.T, lower=True)  19.7 us
    dot_general x1, matrix products, per_device(): jnp.dot(lax.all_gather(embeddings, 'feat', axis=0, tiled=True), freqs, pr...  18.1 us
  transfers between devices with their start and end apart: 3, of which 3 were waited for; matrix products, arithmetic and copies ran while one was open for 0% of the time, Pallas kernels for 0%

profile of v1, /device:TPU:0, one launch (start us, length us, event | category | flops | bytes accessed | tf_op | source)
XLA Modules:
  0.0 581.1 jit_solution(59395947410067255)
XLA Ops:
  7.2 0.0 reduce-scatter.2.cloned.1.call-start
  7.2 32.7 %all_gather.12 = bf16[128,1024]{1,0:T(8,128)(2,1)S(1)} all-gather(bf16[16,1024]{1,0:T(8,128)(2,1)} %param.4), channel_id=1, replica_groups=mesh['rows'=4,'feat'=8] {'feat'}, dimensions={0}, use_global_device_ids=true | all-gather | bytes 294912 | tf_op jit(solution)/shard_map/all_gather | solution.py:11
  39.9 0.0 copy-start
  40.0 18.1 %fusion.1 = bf16[128,8192]{1,0:T(8,128)(2,1)S(1)} fusion(bf16[128,1024]{1,0:T(8,128)(2,1)S(1)} %all_gather.12, bf16[1024,8192]{1,0:T(8,128)(2,1)} %param.5, f32[8192]{0:T(1024)} %param.6), kind=kOutput, calls=%fused_computation.4 | convolution fusion | flops 2149580800 | bytes 19169280 | tf_op jit(solution)/shard_map/dot_general | solution.py:10
  58.1 0.0 copy-done
  58.1 1.5 fusion.12
  59.6 0.0 reduce-scatter.2.cloned.1.call-update
  59.6 0.0 all-reduce.3.cloned.1.call-start
  59.6 62.0 %reduce-scatter.2.cloned.1.call-done = f32[16,256]{1,0:T(8,128)} async-done(((f32[128,256]{1,0:T(8,128)}), f32[16,256]{1,0:T(8,128)}) %reduce-scatter.2.cloned.1.call-update) | async-done | bytes 16400 | tf_op jit(solution)/shard_map/reduce_scatter | solution.py:16
  121.6 0.0 copy-start.1
  121.6 1.9 fusion.13
  123.6 0.0 all-reduce.3.cloned.1.call-update
  123.6 0.2 all-gather.3.cloned.1.call-start
  123.8 128.0 %all-reduce.3.cloned.1.call-done = f32[256,256]{0,1:T(8,128)} async-done(((f32[256,256]{0,1:T(8,128)}), f32[256,256]{0,1:T(8,128)}) %all-reduce.3.cloned.1.call-update) | async-done | bytes 262160 | tf_op jit(solution)/shard_map/psum | solution.py:23
  251.8 1.0 broadcast_multiply_fusion.1
  252.8 0.1 copy.7
  252.9 1.0 fusion.2
  253.9 11.7 %cholesky.50 = f32[128,128]{1,0:T(8,128)S(1)} custom-call(f32[128,128]{1,0:T(8,128)S(1)} %cholesky.118), custom_call_target="Cholesky" | custom-call | tf_op jit(solution)/shard_map/jit(cholesky)/cholesky | solution.py:24
  265.7 9.8 %custom-call.15 = f32[1,128,128]{1,2,0:T(8,128)S(1)} custom-call(f32[1,128,128]{2,1,0:T(8,128)S(1)} %get-tuple-element.25), custom_call_target="InvertDiagBlocksLowerTriangular" | custom-call | tf_op jit(solution)/shard_map/jit(cholesky)/cholesky | solution.py:24
  275.5 0.2 constant_dynamic-update-slice_fusion.1
  275.7 0.3 convolution_subtract_fusion
  276.0 11.7 %cholesky.105 = f32[128,128]{1,0:T(8,128)S(1)} custom-call(f32[128,128]{1,0:T(8,128)S(1)} %convolution_subtract_fusion), custom_call_target="Cholesky" | custom-call | tf_op jit(solution)/shard_map/jit(cholesky)/cholesky | solution.py:24
  287.8 0.7 compare_reduce_fusion
  289.9 0.1 triangular_solve.57
  289.9 4.3 while.1
  290.1 0.6 fusion.28
  290.7 1.4 bitcast_dynamic-update-slice_fusion.2
  292.2 0.6 fusion.28
  292.8 1.4 bitcast_dynamic-update-slice_fusion.2
  294.2 19.7 %custom-call.16 = f32[2,128,128]{1,2,0:T(8,128)S(1)} custom-call(f32[2,128,128]{2,1,0:T(8,128)S(1)} %get-tuple-element.9), custom_call_target="InvertDiagBlocksLowerTriangular" | custom-call | tf_op jit(solution)/shard_map/jit(_solve_triangular)/triangular_solve | solution.py:25
  313.9 0.0 copy-done.1
  313.9 0.2 fusion.5
  314.1 0.2 convolution_subtract_fusion.1
  314.3 0.2 fusion.4
  314.5 0.6 fusion.10
  315.1 30.5 %all_gather.13 = bf16[128,256]{1,0:T(8,128)(2,1)S(1)} all-gather(bf16[16,256]{1,0:T(8,128)(2,1)S(1)} %get-tuple-element.18), channel_id=1, replica_groups=mesh['rows'=4,'feat'=8] {'feat'}, dimensions={0}, use_global_device_ids=true | all-gather | bytes 73728 | tf_op jit(solution)/shard_map/all_gather | solution.py:26
  345.6 4.7 fusion.14
  350.3 0.0 all-gather.3.cloned.1.call-update
  350.3 200.7 %all-gather.3.cloned.1.call-done = f32[1024,8192]{1,0:T(8,128)} async-done(((f32[256,8192]{1,0:T(8,128)}), f32[1024,8192]{1,0:T(8,128)}) %all-gather.3.cloned.1.call-update) | async-done | bytes 33554448 | tf_op jit(solution)/shard_map/all_gather | solution.py:32
  551.0 15.9 %reduce_sum.9 = f32[256,8192]{1,0:T(8,128)} reduce(f32[4,256,8192]{2,1,0:T(8,128)} %bitcast.44, f32[]{:T(128)} %constant.81.clone.1), dimensions={0}, to_apply=%region_6.7 | reduce | flops 6291456 | bytes 41943044 | tf_op jit(solution)/shard_map/reduce_sum | solution.py:33
  566.8 7.7 %broadcast_multiply_fusion = f32[256,8192]{1,0:T(8,128)} fusion(f32[256,8192]{1,0:T(8,128)} %reduce_sum.9), kind=kLoop, calls=%fused_computation.5 | loop fusion | flops 2097152 | bytes 16777216 | tf_op jit(solution)/shard_map/div | solution.py:35
  (9 shorter events, 0.1 us)
Async XLA Ops:
  7.2 114.5 %reduce-scatter.2.cloned.1.call-start = ((), (), s32[]{:S(2)}) async-start(), calls=%async_computation.1 | async-start | bytes 147456 | tf_op jit(solution)/shard_map/reduce_scatter | solution.py:16
  39.9 18.2 %copy-start = (bf16[8192,256]{1,0:T(8,128)(2,1)S(1)}, bf16[8192,256]{1,0:T(8,128)(2,1)}, u32[]{:S(2)}) copy-start(bf16[8192,256]{1,0:T(8,128)(2,1)} %param.7) | copy-start | bytes 12582916
  59.6 192.2 %all-reduce.3.cloned.1.call-start = ((), (), s32[]{:S(2)}) async-start(), calls=%async_computation.2 | async-start | bytes 524288 | tf_op jit(solution)/shard_map/psum | solution.py:23
  121.6 192.3 %copy-start.1 = (f32[16,256]{1,0:T(8,128)S(1)}, f32[16,256]{1,0:T(8,128)}, u32[]{:S(2)}) copy-start(f32[16,256]{1,0:T(8,128)} %reduce-scatter.2.cloned.1.call-done) | copy-start | bytes 49156
  123.6 427.4 %all-gather.3.cloned.1.call-start = ((), (), s32[]{:S(2)}) async-start(), calls=%async_computation.3 | async-start | bytes 41943040 | tf_op jit(solution)/shard_map/all_gather | solution.py:32
Sparse Core Ops, SparseCore 0:
  59.7 61.8 reduce-scatter.1
  127.7 124.0 all-reduce.2
  350.4 200.5 all-gather.2
